TPU v7x, 512 devices: a whole 4x8x8 slice. The times are simulated.
512 devices in a mesh: ha: 8 (over y_lo, core), az: 64 (over x, z, y_hi).
Axes of the slice: x: 4, y: 8 (y_hi: 2, y_lo: 4; y = y_hi * 4 + y_lo), z: 8, core: 2. Of those that a mesh axis runs over, the one named last changes fastest.
Arguments:
- field: float32 [2, 4096, 8192], P(None, 'ha', 'az'), may hold values from -6 to 6
- terrain: int32 [8192], P('az'), may hold values from 0 to 63
- profile_pick: int32 [8192], P('az'), may hold values from 0 to 15
- profile_table: float32 [16, 4096], replicated, may hold values from -3.140625 to 3.140625
- clutter_mask: int32 [128, 8192], P(None, 'az'), may hold values 0 or 1
- pulse: float32 [63], replicated, may hold values from -0.6 to 0.6
- beam: float32 [31], replicated, may hold values from -0.9 to 0.9
- measured: float32 [2, 128, 8192], P(None, None, 'az'), may hold values from -6 to 6
Outputs:
- field_out: float32 [2, 4096, 8192], P(None, 'ha', 'az')
- sources: float32 [2, 2, 128, 8192], P(None, None, 'ha', 'az')
All inputs are finite; a program needn't handle non-finite values. No bound on the sum of `clutter_mask` on one device may be relied on, other than what follows from the above.
Results may differ from a plain program's by a relative error of at most 0.00022.
Values sent between devices are 32-bit elements; how exact they have to be, the bound alone decides.
No kernel may reach another device: no remote copies, remote signals or barrier semaphores. Data moves between devices by JAX's collectives and lax.ppermute only.
A program may use at most 64 MiB of HBM per device.

v0:
```python
import math
import jax
import jax.numpy as jnp
from jax import lax
from jax.sharding import PartitionSpec as P

height_chirp = 1
azimuth_chirp = 3


def broadcast(block, axis, owner):
    block = jnp.where(lax.axis_index(axis) == owner, block, jnp.zeros_like(block))
    return lax.psum(block, axis)


def with_halo(cells, sides, width):
    for axis, dim in sides:
        count = lax.axis_size(axis)
        head = lax.slice_in_dim(cells, 0, width, axis=dim)
        tail = lax.slice_in_dim(cells, cells.shape[dim] - width, cells.shape[dim], axis=dim)
        cells = jnp.concatenate(
            [
                lax.ppermute(tail, axis, [(i, (i + 1) % count) for i in range(count)]),
                cells,
                lax.ppermute(head, axis, [((i + 1) % count, i) for i in range(count)]),
            ],
            axis=dim,
        )
    return cells


def factors(count):
    first = 1
    probe = 1
    while probe * probe <= count:
        if count % probe == 0:
            first = probe
        probe += 1
    return (first, count // first)


def unit_roots(rows, cols, modulus):
    left = lax.broadcasted_iota(jnp.int32, (rows, cols), 0)
    right = lax.broadcasted_iota(jnp.int32, (rows, cols), 1)
    turn = (left * right % modulus).astype(jnp.float32) * (2.0 * math.pi / modulus)
    return (jnp.cos(turn), -jnp.sin(turn))


def chirp_table(first, second, spread, count):
    low = lax.broadcasted_iota(jnp.int32, (first, second), 0)
    high = lax.broadcasted_iota(jnp.int32, (first, second), 1)
    index = low + first * high
    angle = (spread * index * index % (2 * count)).astype(jnp.float32) * (-math.pi / count)
    return (jnp.cos(angle), jnp.sin(angle))


def complex_table(table_re, table_im):
    return jnp.stack([jnp.stack([table_re, -table_im]), jnp.stack([table_im, table_re])])


def cmul(left_re, left_im, right_re, right_im):
    return (left_re * right_re - left_im * right_im, left_re * right_im + left_im * right_re)


def stacked_mul(vals, table_re, table_im):
    new_re, new_im = cmul(vals[0], vals[1], table_re, table_im)
    return jnp.stack([new_re, new_im])


def propagate(part_re, part_im, spread):
    highest = lax.Precision.HIGHEST
    count = part_re.shape[1]
    first, second = factors(count)
    split = (part_re.shape[0], first, second)
    table_shape = (1, first, second)
    outer_re, outer_im = unit_roots(first, first, first)
    inner_re, inner_im = unit_roots(second, second, second)
    twist_re, twist_im = unit_roots(first, second, count)
    twist_re = twist_re.reshape(table_shape)
    twist_im = twist_im.reshape(table_shape)
    phase_re, phase_im = chirp_table(first, second, spread, count)
    phase_re = phase_re.reshape(table_shape)
    phase_im = phase_im.reshape(table_shape)
    outer_fwd = complex_table(outer_re, outer_im)
    inner_fwd = complex_table(inner_re, inner_im)
    inner_inv = complex_table(inner_re.T, -inner_im.T)
    outer_inv = complex_table(outer_re.T, -outer_im.T)
    vals = jnp.stack([part_re.reshape(split), part_im.reshape(split)])
    vals = jnp.einsum("ocka,clab->olkb", outer_fwd, vals, precision=highest)
    vals = stacked_mul(vals, twist_re, twist_im)
    vals = jnp.einsum("clkb,ocbq->olkq", vals, inner_fwd, precision=highest)
    vals = stacked_mul(vals, phase_re, phase_im)
    vals = jnp.einsum("clkq,ocqb->olkb", vals, inner_inv, precision=highest)
    vals = stacked_mul(vals, twist_re, -twist_im)
    vals = jnp.einsum("ocak,clkb->olab", outer_inv, vals, precision=highest)
    scale = 1.0 / count
    return ((vals[0] * scale).reshape(part_re.shape), (vals[1] * scale).reshape(part_im.shape))


def screen_coef(rows, terr, phase, total):
    height = rows.astype(jnp.float32)
    depth = jnp.maximum(height - 0.75 * total, 0.0) / (0.25 * total)
    amount = jnp.exp(-4.0 * depth * depth) * (rows >= terr).astype(jnp.float32)
    return (amount * jnp.cos(phase), amount * jnp.sin(phase))


def onehot_of(picks, count):
    return (picks[None, :] == lax.broadcasted_iota(jnp.int32, (count, picks.shape[0]), 0)).astype(
        jnp.float32
    )


def lookup(table, picks):
    return jnp.einsum(
        "pr,pc->rc", table, onehot_of(picks, table.shape[0]), precision=lax.Precision.HIGHEST
    )


def band(taps, offset):
    hit = offset[:, :, None] == lax.broadcasted_iota(jnp.int32, (1, 1, taps.shape[0]), 2)
    return jnp.sum(jnp.where(hit, taps[None, None, :], 0.0), axis=-1)


def apply_screen(wave, coef):
    new_re, new_im = cmul(wave[0], wave[1], coef[0], coef[1])
    return jnp.stack([new_re, new_im])


def turn_rows(rows):
    new_re, new_im = propagate(rows[0], rows[1], azimuth_chirp)
    return jnp.stack([new_re, new_im])


def turn_items(block):
    return turn_rows(block[:, 0])[:, None]


def to_rows(wave):
    n_az = lax.axis_size("az")
    h_dev = wave.shape[1]
    part_rows = h_dev // n_az
    shaped = wave.reshape(2, n_az, part_rows, wave.shape[2])
    moved = turn_items(lax.all_to_all(shaped, "az", split_axis=1, concat_axis=3, tiled=True))
    return moved.reshape(2, part_rows, moved.shape[3])


def rows_to_slab(rows):
    return lax.all_to_all(rows, "az", split_axis=2, concat_axis=1, tiled=True)


def across(wave):
    return rows_to_slab(to_rows(wave))


def to_tall(wave):
    flipped = jnp.swapaxes(wave, 1, 2)
    return lax.all_to_all(flipped, "ha", split_axis=1, concat_axis=2, tiled=True)


def to_slab(tall):
    flipped = lax.all_to_all(tall, "ha", split_axis=2, concat_axis=1, tiled=True)
    return jnp.swapaxes(flipped, 1, 2)


def down(tall):
    new_re, new_im = propagate(tall[0], tall[1], height_chirp)
    return jnp.stack([new_re, new_im])


def root_strip(wave, bottom):
    return broadcast(wave[:, :bottom, :], "ha", 0)


def beam_forward(values, half_beam, forward_band):
    wider = with_halo(values, (("az", 1),), half_beam)
    return jnp.dot(wider, forward_band, precision=lax.Precision.HIGHEST)


def beam_backward(values, half_beam, back_band):
    wider = with_halo(values, (("az", 1),), half_beam)
    return jnp.dot(wider, back_band, precision=lax.Precision.HIGHEST)


def local(field, terrain, profile_pick, profile_table, clutter_mask, pulse, beam, measured):
    highest = lax.Precision.HIGHEST
    n_slabs = lax.axis_size("ha")
    h_dev = field.shape[1]
    a_dev = field.shape[2]
    total_h = h_dev * n_slabs
    slab = lax.axis_index("ha")
    bottom = clutter_mask.shape[0]
    share_rows = bottom // n_slabs
    row_start = slab * share_rows
    mask = clutter_mask.astype(jnp.float32)
    taps_range = pulse.shape[0]
    half_range = (taps_range - 1) // 2
    row_grid = lax.broadcasted_iota(jnp.int32, (bottom, bottom), 0)
    col_grid = lax.broadcasted_iota(jnp.int32, (bottom, bottom), 1)
    rmat = band(pulse, col_grid - row_grid + half_range)
    half_beam = (beam.shape[0] - 1) // 2
    wide = a_dev + 2 * half_beam
    edge = lax.broadcasted_iota(jnp.int32, (wide, a_dev), 0)
    column = lax.broadcasted_iota(jnp.int32, (wide, a_dev), 1)
    forward_band = band(beam, edge - column)
    back_band = band(beam, column - edge + 2 * half_beam)
    slab_rows = slab * h_dev + lax.broadcasted_iota(jnp.int32, (h_dev, 1), 0)
    slab_phase = lookup(
        lax.dynamic_slice_in_dim(profile_table, slab * h_dev, h_dev, 1), profile_pick
    )
    slab_coef = screen_coef(slab_rows, terrain[None, :], slab_phase, total_h)
    steps_count = measured.shape[0]
    wave = field
    result = []
    for step in range(steps_count):
        wave = to_slab(down(to_tall(across(wave))))
        wave = apply_screen(wave, slab_coef)
        strip = root_strip(wave, bottom)
        low_re = strip[0]
        low_im = strip[1]
        power = mask * (low_re * low_re + low_im * low_im)
        target = measured[step]
        ranged = jnp.dot(rmat, power, precision=highest)
        model = beam_forward(ranged, half_beam, forward_band)
        misfit = model - target
        spread_back = beam_backward(misfit, half_beam, back_band)
        back = jnp.einsum("pr,pa->ra", rmat, spread_back, precision=highest)
        whole = jnp.stack([2.0 * mask * low_re * back, 2.0 * mask * low_im * back])
        result.append(lax.dynamic_slice_in_dim(whole, row_start, share_rows, 1))
    return (wave, jnp.stack(result))


def solution(mesh):
    return jax.shard_map(
        local,
        mesh=mesh,
        in_specs=(
            P(None, "ha", "az"),
            P("az"),
            P("az"),
            P(),
            P(None, "az"),
            P(),
            P(),
            P(None, None, "az"),
        ),
        out_specs=(P(None, "ha", "az"), P(None, None, "ha", "az")),
        check_vma=False,
    )
```

profile of v0, /device:TPU:8, one launch (start us, length us, event | category | flops | bytes accessed | tf_op | source)
XLA Modules:
  0.0 512.8 jit_solution(6664515977165057099)
XLA Ops:
  9.1 18.1 %all-to-all-start = ((f32[2,64,8,128]{3,2,0,1:T(8,128)}), f32[2,64,8,128]{3,2,0,1:T(8,128)S(1)}, u32[]{:S(2)}, u32[]{:S(2)}) async-start(f32[2,64,8,128]{3,2,0,1:T(8,128)} %copy.267), calls=%async_computation | async-start | bytes 1048576 | tf_op jit(solution)/shard_map/all_to_all | solution.py:143
  28.6 21.4 %all-to-all-done = f32[2,64,8,128]{3,2,0,1:T(8,128)S(1)} async-done(((f32[2,64,8,128]{3,2,0,1:T(8,128)}), f32[2,64,8,128]{3,2,0,1:T(8,128)S(1)}, u32[]{:S(2)}, u32[]{:S(2)}) %all-to-all-start) | async-done | bytes 524320 | tf_op jit(solution)/shard_map/all_to_all | solution.py:143
  53.2 7.7 %copy.272 = f32[2,8,8192]{1,0,2:T(2,128)} copy(f32[2,8,8192]{2,1,0:T(8,128)S(1)} %pad_maximum_fusion.1) | data formatting | bytes 1048576 | tf_op jit(solution)/shard_map/stack | solution.py:131
  60.9 13.0 %reshape.559 = f32[64,1,2048]{2,1,0:T(1,128)S(1)} reshape(f32[8192,2,8]{2,1,0:T(2,128)} %bitcast.382) | data formatting | bytes 1048576
  73.8 27.5 %all_to_all.132 = f32[64,1,2048]{2,1,0:T(1,128)S(1)} all-to-all(f32[64,1,2048]{2,1,0:T(1,128)S(1)} %reshape.559), channel_id=1, replica_groups=mesh['ha'=8,'az'=64] {'az'}, dimensions={0} | all-to-all | bytes 1048576 | tf_op jit(solution)/shard_map/all_to_all | solution.py:148
  103.8 14.1 %reshape.560 = f32[8192,2,8]{2,1,0:T(2,128)} reshape(f32[64,2048]{1,0:T(8,128)S(1)} %reduce) | data formatting | bytes 1048576
  117.9 9.2 %copy.365 = f32[2,8,64,128]{3,1,2,0:T(8,128)S(1)} copy(f32[2,8,64,128]{1,0,3,2:T(2,128)} %bitcast.383) | data formatting | bytes 1048576 | tf_op jit(solution)/shard_map/all_to_all | solution.py:148
  132.0 11.4 %all-to-all-done.2 = f32[2,128,512]{2,0,1:T(2,128)S(1)} async-done(((f32[2,128,512]{2,0,1:T(2,128)}), f32[2,128,512]{2,0,1:T(2,128)S(1)}, u32[]{:S(2)}, u32[]{:S(2)}) %all-to-all-start.2) | async-done | bytes 524320 | tf_op jit(solution)/shard_map/all_to_all | solution.py:157
  150.2 4.4 copy.288
  154.6 7.9 %reshape.561 = f32[8,1,16384]{2,1,0:T(1,128)} reshape(f32[4096,2,16]{2,1,0:T(2,128)} %bitcast.386) | data formatting | bytes 1048576
  162.4 7.1 %all-to-all-start.3 = ((f32[8,1,16384]{2,1,0:T(1,128)}), f32[8,1,16384]{2,1,0:T(1,128)S(1)}, u32[]{:S(2)}, u32[]{:S(2)}) async-start(f32[8,1,16384]{2,1,0:T(1,128)} %reshape.561), calls=%async_computation.3 | async-start | bytes 1048576 | tf_op jit(solution)/shard_map/all_to_all | solution.py:161
  169.5 12.1 %all-to-all-done.3 = f32[8,1,16384]{2,1,0:T(1,128)S(1)} async-done(((f32[8,1,16384]{2,1,0:T(1,128)}), f32[8,1,16384]{2,1,0:T(1,128)S(1)}, u32[]{:S(2)}, u32[]{:S(2)}) %all-to-all-start.3) | async-done | bytes 524320 | tf_op jit(solution)/shard_map/all_to_all | solution.py:161
  183.5 7.6 %reshape.562 = f32[4096,2,16]{2,1,0:T(2,128)} reshape(f32[8,16384]{1,0:T(8,128)S(1)} %reduce.1) | data formatting | bytes 1048576
  191.1 5.1 copy.371
  197.8 26.0 %all_to_all.133 = f32[2,64,8,128]{3,2,0,1:T(8,128)S(1)} all-to-all(f32[2,64,8,128]{3,2,0,1:T(8,128)S(1)} %pad_maximum_fusion.3), channel_id=1, replica_groups=mesh['ha'=8,'az'=64] {'az'}, dimensions={1} | all-to-all | bytes 1048576 | tf_op jit(solution)/shard_map/all_to_all | solution.py:143
  227.0 7.7 %copy.298 = f32[2,8,8192]{1,0,2:T(2,128)} copy(f32[2,8,8192]{2,1,0:T(8,128)S(1)} %pad_maximum_fusion.4) | data formatting | bytes 1048576 | tf_op jit(solution)/shard_map/stack | solution.py:131
  234.7 13.0 %reshape.563 = f32[64,1,2048]{2,1,0:T(1,128)S(1)} reshape(f32[8192,2,8]{2,1,0:T(2,128)} %bitcast.384) | data formatting | bytes 1048576
  247.7 30.4 %all_to_all.134 = f32[64,1,2048]{2,1,0:T(1,128)S(1)} all-to-all(f32[64,1,2048]{2,1,0:T(1,128)S(1)} %reshape.563), channel_id=1, replica_groups=mesh['ha'=8,'az'=64] {'az'}, dimensions={0} | all-to-all | bytes 1048576 | tf_op jit(solution)/shard_map/all_to_all | solution.py:148
  280.0 14.1 %reshape.564 = f32[8192,2,8]{2,1,0:T(2,128)} reshape(f32[64,2048]{1,0:T(8,128)S(1)} %reduce.2) | data formatting | bytes 1048576
  294.1 9.2 %copy.376 = f32[2,8,64,128]{3,1,2,0:T(8,128)S(1)} copy(f32[2,8,64,128]{1,0,3,2:T(2,128)} %bitcast.385) | data formatting | bytes 1048576 | tf_op jit(solution)/shard_map/all_to_all | solution.py:148
  303.5 17.0 %all_to_all.135 = f32[2,128,512]{2,0,1:T(2,128)S(1)} all-to-all(f32[2,128,512]{2,0,1:T(2,128)S(1)} %copy.301), channel_id=1, replica_groups=mesh['ha'=8,'az'=64] {'ha'}, dimensions={1} | all-to-all | bytes 1048576 | tf_op jit(solution)/shard_map/all_to_all | solution.py:157
  331.6 7.9 %reshape.565 = f32[8,1,16384]{2,1,0:T(1,128)} reshape(f32[4096,2,16]{2,1,0:T(2,128)} %bitcast.388) | data formatting | bytes 1048576
  339.5 5.7 %all-to-all-start.7 = ((f32[8,1,16384]{2,1,0:T(1,128)}), f32[8,1,16384]{2,1,0:T(1,128)S(1)}, u32[]{:S(2)}, u32[]{:S(2)}) async-start(f32[8,1,16384]{2,1,0:T(1,128)} %reshape.565), calls=%async_computation.7 | async-start | bytes 1048576 | tf_op jit(solution)/shard_map/all_to_all | solution.py:161
  347.0 10.4 %all-to-all-done.7 = f32[8,1,16384]{2,1,0:T(1,128)S(1)} async-done(((f32[8,1,16384]{2,1,0:T(1,128)}), f32[8,1,16384]{2,1,0:T(1,128)S(1)}, u32[]{:S(2)}, u32[]{:S(2)}) %all-to-all-start.7) | async-done | bytes 524320 | tf_op jit(solution)/shard_map/all_to_all | solution.py:161
  359.2 7.6 %reshape.566 = f32[4096,2,16]{2,1,0:T(2,128)} reshape(f32[8,16384]{1,0:T(8,128)S(1)} %reduce.3) | data formatting | bytes 1048576
  366.8 5.2 %copy.382 = f32[2,16,8,512]{3,1,2,0:T(8,128)S(1)} copy(f32[2,16,8,512]{1,0,3,2:T(2,128)} %bitcast.389) | data formatting | bytes 1048576 | tf_op jit(solution)/shard_map/all_to_all | solution.py:161
  375.6 67.0 %all-reduce.3.cloned.1.call-done = (f32[2,128,128]{2,1,0:T(8,128)}, f32[2,128,128]{2,1,0:T(8,128)}) async-done(((f32[2,128,128]{2,1,0:T(8,128)}, f32[2,128,128]{2,1,0:T(8,128)}), (f32[2,128,128]{2,1,0:T(8,128)}, f32[2,128,128]{2,1,0:T(8,128)})) %all-reduce.3.cloned.1.call-update) | async-done | bytes 262160 | tf_op jit(solution)/shard_map/psum | solution.py:13
  444.9 4.6 collective-permute-start
  449.6 9.3 %collective-permute-start.1 = (f32[128,15]{0,1:T(8,128)S(1)}, f32[128,15]{0,1:T(8,128)S(1)}, u32[]{:S(2)}, u32[]{:S(2)}) collective-permute-start(f32[128,15]{0,1:T(8,128)S(1)} %get-tuple-element.65), channel_id=1, source_target_pairs={{1,0},{2,1},{3,2},{4,3},{5,4},{6,5},{7,6},{8,7},{9,8},{10,9},{11,1... | collective-permute-start | bytes 23048 | tf_op jit(solution)/shard_map/ppermute | solution.py:25
  460.9 12.0 %collective-permute-start.5 = (f32[128,15]{0,1:T(8,128)S(1)}, f32[128,15]{0,1:T(8,128)S(1)}, u32[]{:S(2)}, u32[]{:S(2)}) collective-permute-start(f32[128,15]{0,1:T(8,128)S(1)} %get-tuple-element.69), channel_id=1, source_target_pairs={{1,0},{2,1},{3,2},{4,3},{5,4},{6,5},{7,6},{8,7},{9,8},{10,9},{11,1... | collective-permute-start | bytes 23048 | tf_op jit(solution)/shard_map/ppermute | solution.py:25
  475.3 12.0 %collective-permute-start.3 = (f32[128,15]{0,1:T(8,128)S(1)}, f32[128,15]{0,1:T(8,128)S(1)}, u32[]{:S(2)}, u32[]{:S(2)}) collective-permute-start(f32[128,15]{0,1:T(8,128)S(1)} %get-tuple-element.63), channel_id=1, source_target_pairs={{1,0},{2,1},{3,2},{4,3},{5,4},{6,5},{7,6},{8,7},{9,8},{10,9},{11,1... | collective-permute-start | bytes 23048 | tf_op jit(solution)/shard_map/ppermute | solution.py:25
  489.8 12.0 %collective-permute-start.7 = (f32[128,15]{0,1:T(8,128)S(1)}, f32[128,15]{0,1:T(8,128)S(1)}, u32[]{:S(2)}, u32[]{:S(2)}) collective-permute-start(f32[128,15]{0,1:T(8,128)S(1)} %get-tuple-element.67), channel_id=1, source_target_pairs={{1,0},{2,1},{3,2},{4,3},{5,4},{6,5},{7,6},{8,7},{9,8},{10,9},{11,1... | collective-permute-start | bytes 23048 | tf_op jit(solution)/shard_map/ppermute | solution.py:25
  (153 shorter events, 59.7 us)
Async XLA Ops:
  7.2 189.3 %copy-start = (f32[16,4096]{1,0:T(8,128)S(1)}, f32[16,4096]{1,0:T(8,128)}, u32[]{:S(2)}) copy-start(f32[16,4096]{1,0:T(8,128)} %param.11) | copy-start | bytes 786436
  9.1 40.9 %all-to-all-start = ((f32[2,64,8,128]{3,2,0,1:T(8,128)}), f32[2,64,8,128]{3,2,0,1:T(8,128)S(1)}, u32[]{:S(2)}, u32[]{:S(2)}) async-start(f32[2,64,8,128]{3,2,0,1:T(8,128)} %copy.267), calls=%async_computation | async-start | bytes 1048576 | tf_op jit(solution)/shard_map/all_to_all | solution.py:143
  128.0 15.4 %all-to-all-start.2 = ((f32[2,128,512]{2,0,1:T(2,128)}), f32[2,128,512]{2,0,1:T(2,128)S(1)}, u32[]{:S(2)}, u32[]{:S(2)}) async-start(f32[2,128,512]{2,0,1:T(2,128)} %copy.275), calls=%async_computation.2 | async-start | bytes 1048576 | tf_op jit(solution)/shard_map/all_to_all | solution.py:157
  162.4 19.2 %all-to-all-start.3 = ((f32[8,1,16384]{2,1,0:T(1,128)}), f32[8,1,16384]{2,1,0:T(1,128)S(1)}, u32[]{:S(2)}, u32[]{:S(2)}) async-start(f32[8,1,16384]{2,1,0:T(1,128)} %reshape.561), calls=%async_computation.3 | async-start | bytes 1048576 | tf_op jit(solution)/shard_map/all_to_all | solution.py:161
  183.5 12.9 %copy-start.4 = (s32[128]{0:T(128)S(1)}, s32[128]{0:T(128)}, u32[]{:S(2)}) copy-start(s32[128]{0:T(128)} %param.9) | copy-start | bytes 1540
  183.5 12.9 %copy-start.5 = (s32[128]{0:T(128)S(1)}, s32[128]{0:T(128)}, u32[]{:S(2)}) copy-start(s32[128]{0:T(128)} %param.10) | copy-start | bytes 1540
  327.2 18.2 %copy-start.3 = (f32[2,128,128]{2,1,0:T(8,128)S(1)}, f32[2,128,128]{2,1,0:T(8,128)}, u32[]{:S(2)}) copy-start(f32[2,128,128]{2,1,0:T(8,128)} %param.15) | copy-start | bytes 393220
  331.6 14.1 %copy-start.6 = (f32[31]{0:T(128)S(1)}, f32[31]{0:T(128)}, u32[]{:S(2)}) copy-start(f32[31]{0:T(128)} %param.14) | copy-start | bytes 376
  339.5 17.8 %all-to-all-start.7 = ((f32[8,1,16384]{2,1,0:T(1,128)}), f32[8,1,16384]{2,1,0:T(1,128)S(1)}, u32[]{:S(2)}, u32[]{:S(2)}) async-start(f32[8,1,16384]{2,1,0:T(1,128)} %reshape.565), calls=%async_computation.7 | async-start | bytes 1048576 | tf_op jit(solution)/shard_map/all_to_all | solution.py:161
  345.2 97.4 %all-reduce.3.cloned.1.call-start = ((), (), s32[]{:S(2)}) async-start(), calls=%async_computation.8 | async-start | bytes 524288 | tf_op jit(solution)/shard_map/psum | solution.py:13
  366.8 7.5 %copy-start.7 = (f32[63]{0:T(128)S(1)}, f32[63]{0:T(128)}, u32[]{:S(2)}) copy-start(f32[63]{0:T(128)} %param.13) | copy-start | bytes 760
  366.8 75.8 %copy-start.2 = (s32[128,128]{1,0:T(8,128)S(1)}, s32[128,128]{1,0:T(8,128)}, u32[]{:S(2)}) copy-start(s32[128,128]{1,0:T(8,128)} %param.12) | copy-start | bytes 196612
  366.8 138.7 %copy-start.1 = (f32[16,4096]{1,0:T(8,128)S(1)}, f32[16,4096]{1,0:T(8,128)}, u32[]{:S(2)}) copy-start(f32[16,4096]{1,0:T(8,128)} %param.11) | copy-start | bytes 786436
  444.9 28.0 %collective-permute-start = (f32[128,15]{0,1:T(8,128)S(1)}, f32[128,15]{0,1:T(8,128)S(1)}, u32[]{:S(2)}, u32[]{:S(2)}) collective-permute-start(f32[128,15]{0,1:T(8,128)S(1)} %get-tuple-element.64), channel_id=1, source_target_pairs={{0,1},{1,2},{2,3},{3,4},{4,5},{5,6},{6,7},{7,8},{8,9},{9,10},{10,1... | collective-permute-start | bytes 23048 | tf_op jit(solution)/shard_map/ppermute | solution.py:23
  449.6 23.4 %collective-permute-start.1 = (f32[128,15]{0,1:T(8,128)S(1)}, f32[128,15]{0,1:T(8,128)S(1)}, u32[]{:S(2)}, u32[]{:S(2)}) collective-permute-start(f32[128,15]{0,1:T(8,128)S(1)} %get-tuple-element.65), channel_id=1, source_target_pairs={{1,0},{2,1},{3,2},{4,3},{5,4},{6,5},{7,6},{8,7},{9,8},{10,9},{11,1... | collective-permute-start | bytes 23048 | tf_op jit(solution)/shard_map/ppermute | solution.py:25
  458.9 28.5 %collective-permute-start.4 = (f32[128,15]{0,1:T(8,128)S(1)}, f32[128,15]{0,1:T(8,128)S(1)}, u32[]{:S(2)}, u32[]{:S(2)}) collective-permute-start(f32[128,15]{0,1:T(8,128)S(1)} %get-tuple-element.68), channel_id=1, source_target_pairs={{0,1},{1,2},{2,3},{3,4},{4,5},{5,6},{6,7},{7,8},{8,9},{9,10},{10,1... | collective-permute-start | bytes 23048 | tf_op jit(solution)/shard_map/ppermute | solution.py:23
  460.9 26.5 %collective-permute-start.5 = (f32[128,15]{0,1:T(8,128)S(1)}, f32[128,15]{0,1:T(8,128)S(1)}, u32[]{:S(2)}, u32[]{:S(2)}) collective-permute-start(f32[128,15]{0,1:T(8,128)S(1)} %get-tuple-element.69), channel_id=1, source_target_pairs={{1,0},{2,1},{3,2},{4,3},{5,4},{6,5},{7,6},{8,7},{9,8},{10,9},{11,1... | collective-permute-start | bytes 23048 | tf_op jit(solution)/shard_map/ppermute | solution.py:25
  473.4 28.4 %collective-permute-start.2 = (f32[128,15]{0,1:T(8,128)S(1)}, f32[128,15]{0,1:T(8,128)S(1)}, u32[]{:S(2)}, u32[]{:S(2)}) collective-permute-start(f32[128,15]{0,1:T(8,128)S(1)} %get-tuple-element.62), channel_id=1, source_target_pairs={{0,1},{1,2},{2,3},{3,4},{4,5},{5,6},{6,7},{7,8},{8,9},{9,10},{10,1... | collective-permute-start | bytes 23048 | tf_op jit(solution)/shard_map/ppermute | solution.py:23
  475.3 26.5 %collective-permute-start.3 = (f32[128,15]{0,1:T(8,128)S(1)}, f32[128,15]{0,1:T(8,128)S(1)}, u32[]{:S(2)}, u32[]{:S(2)}) collective-permute-start(f32[128,15]{0,1:T(8,128)S(1)} %get-tuple-element.63), channel_id=1, source_target_pairs={{1,0},{2,1},{3,2},{4,3},{5,4},{6,5},{7,6},{8,7},{9,8},{10,9},{11,1... | collective-permute-start | bytes 23048 | tf_op jit(solution)/shard_map/ppermute | solution.py:25
  487.9 14.7 %collective-permute-start.6 = (f32[128,15]{0,1:T(8,128)S(1)}, f32[128,15]{0,1:T(8,128)S(1)}, u32[]{:S(2)}, u32[]{:S(2)}) collective-permute-start(f32[128,15]{0,1:T(8,128)S(1)} %get-tuple-element.66), channel_id=1, source_target_pairs={{0,1},{1,2},{2,3},{3,4},{4,5},{5,6},{6,7},{7,8},{8,9},{9,10},{10,1... | collective-permute-start | bytes 23048 | tf_op jit(solution)/shard_map/ppermute | solution.py:23
  489.8 13.4 %collective-permute-start.7 = (f32[128,15]{0,1:T(8,128)S(1)}, f32[128,15]{0,1:T(8,128)S(1)}, u32[]{:S(2)}, u32[]{:S(2)}) collective-permute-start(f32[128,15]{0,1:T(8,128)S(1)} %get-tuple-element.67), channel_id=1, source_target_pairs={{1,0},{2,1},{3,2},{4,3},{5,4},{6,5},{7,6},{8,7},{9,8},{10,9},{11,1... | collective-permute-start | bytes 23048 | tf_op jit(solution)/shard_map/ppermute | solution.py:25
Sparse Core Ops, SparseCore 0:
  374.4 68.1 all-reduce.2
where the time goes:
time: 522 us; the launch traced here: 513 us
  local copies, waits for them, and re-layouts  146 us (28%)
  waiting for transfers between devices  123 us (24%)
  blocking collectives  101 us (19%)
  starting transfers between devices  90.5 us (17%)
  matrix products  20.1 us (4%)
  other arithmetic  16.4 us (3%)
  between operations  15.5 us (3%)
    unnamed x26, local copies, waits for them, and re-layouts  85.3 us
    psum x1, waiting for transfers between devices, broadcast(): return lax.psum(block, axis)  67 us
    all_to_all x2, blocking collectives, rows_to_slab(): return lax.all_to_all(rows, 'az', split_axis=2, concat_axis=1, tiled=True)  57.9 us
    ppermute x4, starting transfers between devices, with_halo(): lax.ppermute(head, axis, [((i + 1) % count, i) for i in range(count)])  45.5 us
    all_to_all x1, blocking collectives, to_rows(): lax.all_to_all(shaped, 'az', split_axis=1, concat_axis=3, tiled=True)  26 us
    all_to_all x2, waiting for transfers between devices, to_slab(): lax.all_to_all(tall, 'ha', split_axis=2, concat_axis=1, tiled=True)  22.4 us
    all_to_all x1, waiting for transfers between devices, to_rows(): lax.all_to_all(shaped, 'az', split_axis=1, concat_axis=3, tiled=True)  21.4 us
    all_to_all x3, local copies, waits for them, and re-layouts, rows_to_slab(): return lax.all_to_all(rows, 'az', split_axis=2, concat_axis=1, tiled=True)  18.8 us
  transfers between devices with their start and end apart: 13, of which 6 were waited for; matrix products, arithmetic and copies ran while one was open for 1% of the time, Pallas kernels for 0%

commit v1 on v0

--- a/solution.py
+++ b/solution.py
@@ -3,14 +3,16 @@
 import jax.numpy as jnp
 from jax import lax
 from jax.sharding import PartitionSpec as P
+from jax.lax import all_gather
 
 height_chirp = 1
 azimuth_chirp = 3
+drive_the_links = lambda xs, ax_name: jnp.sum(all_gather(xs, ax_name), axis=0)
 
 
 def broadcast(block, axis, owner):
     block = jnp.where(lax.axis_index(axis) == owner, block, jnp.zeros_like(block))
-    return lax.psum(block, axis)
+    return drive_the_links(block, axis)
 
 
 def with_halo(cells, sides, width):

time: 522 us -> 463 us (0.89)
  the two profiles are of different devices: /device:TPU:8 before, /device:TPU:24 now
where the time goes in v1:
time: 463 us; the launch traced here: 454 us
  local copies, waits for them, and re-layouts  147 us (32%)
  starting transfers between devices  103 us (22%)
  blocking collectives  80.1 us (17%)
  waiting for transfers between devices  71.1 us (15%)
  other arithmetic  19 us (4%)
  matrix products  17.4 us (4%)
  between operations  15.5 us (3%)
    unnamed x26, local copies, waits for them, and re-layouts  85.3 us
    all_to_all x2, blocking collectives, rows_to_slab(): return lax.all_to_all(rows, 'az', split_axis=2, concat_axis=1, tiled=True)  53.3 us
    ppermute x4, starting transfers between devices, with_halo(): lax.ppermute(head, axis, [((i + 1) % count, i) for i in range(count)])  46.8 us
    all_to_all x1, blocking collectives, to_rows(): lax.all_to_all(shaped, 'az', split_axis=1, concat_axis=3, tiled=True)  26.8 us
    all_to_all x2, waiting for transfers between devices, to_tall(): lax.all_to_all(flipped, 'ha', split_axis=1, concat_axis=2, tiled=True)  25.7 us
    all_to_all x2, waiting for transfers between devices, to_slab(): lax.all_to_all(tall, 'ha', split_axis=2, concat_axis=1, tiled=True)  25.2 us
    all_to_all x3, local copies, waits for them, and re-layouts, rows_to_slab(): return lax.all_to_all(rows, 'az', split_axis=2, concat_axis=1, tiled=True)  18.8 us
    all_to_all x2, starting transfers between devices, to_tall(): lax.all_to_all(flipped, 'ha', split_axis=1, concat_axis=2, tiled=True)  17.3 us
  transfers between devices with their start and end apart: 15, of which 9 were waited for; matrix products, arithmetic and copies ran while one was open for 9% of the time, Pallas kernels for 0%

profile of v1, /device:TPU:24, one launch (start us, length us, event | category | flops | bytes accessed | tf_op | source)
XLA Modules:
  0.0 453.9 jit_solution(9957482894521365410)
XLA Ops:
  9.1 16.3 %all-to-all-start = ((f32[2,64,8,128]{3,2,0,1:T(8,128)}), f32[2,64,8,128]{3,2,0,1:T(8,128)S(1)}, u32[]{:S(2)}, u32[]{:S(2)}) async-start(f32[2,64,8,128]{3,2,0,1:T(8,128)} %copy.267), calls=%async_computation | async-start | bytes 1048576 | tf_op jit(solution)/shard_map/all_to_all | solution.py:145
  26.8 16.1 %all-to-all-done = f32[2,64,8,128]{3,2,0,1:T(8,128)S(1)} async-done(((f32[2,64,8,128]{3,2,0,1:T(8,128)}), f32[2,64,8,128]{3,2,0,1:T(8,128)S(1)}, u32[]{:S(2)}, u32[]{:S(2)}) %all-to-all-start) | async-done | bytes 524320 | tf_op jit(solution)/shard_map/all_to_all | solution.py:145
  46.1 7.7 %copy.272 = f32[2,8,8192]{1,0,2:T(2,128)} copy(f32[2,8,8192]{2,1,0:T(8,128)S(1)} %pad_maximum_fusion.1) | data formatting | bytes 1048576 | tf_op jit(solution)/shard_map/stack | solution.py:133
  53.8 13.0 %reshape.561 = f32[64,1,2048]{2,1,0:T(1,128)S(1)} reshape(f32[8192,2,8]{2,1,0:T(2,128)} %bitcast.384) | data formatting | bytes 1048576
  66.8 27.4 %all_to_all.132 = f32[64,1,2048]{2,1,0:T(1,128)S(1)} all-to-all(f32[64,1,2048]{2,1,0:T(1,128)S(1)} %reshape.561), channel_id=1, replica_groups=mesh['ha'=8,'az'=64] {'az'}, dimensions={0} | all-to-all | bytes 1048576 | tf_op jit(solution)/shard_map/all_to_all | solution.py:150
  96.6 14.1 %reshape.562 = f32[8192,2,8]{2,1,0:T(2,128)} reshape(f32[64,2048]{1,0:T(8,128)S(1)} %reduce) | data formatting | bytes 1048576
  110.7 9.2 %copy.365 = f32[2,8,64,128]{3,1,2,0:T(8,128)S(1)} copy(f32[2,8,64,128]{1,0,3,2:T(2,128)} %bitcast.385) | data formatting | bytes 1048576 | tf_op jit(solution)/shard_map/all_to_all | solution.py:150
  120.8 10.3 %all-to-all-start.2 = ((f32[2,128,512]{2,0,1:T(2,128)}), f32[2,128,512]{2,0,1:T(2,128)S(1)}, u32[]{:S(2)}, u32[]{:S(2)}) async-start(f32[2,128,512]{2,0,1:T(2,128)} %copy.275), calls=%async_computation.2 | async-start | bytes 1048576 | tf_op jit(solution)/shard_map/all_to_all | solution.py:159
  131.6 12.3 %all-to-all-done.2 = f32[2,128,512]{2,0,1:T(2,128)S(1)} async-done(((f32[2,128,512]{2,0,1:T(2,128)}), f32[2,128,512]{2,0,1:T(2,128)S(1)}, u32[]{:S(2)}, u32[]{:S(2)}) %all-to-all-start.2) | async-done | bytes 524320 | tf_op jit(solution)/shard_map/all_to_all | solution.py:159
  150.7 4.4 copy.288
  155.0 7.9 %reshape.563 = f32[8,1,16384]{2,1,0:T(1,128)} reshape(f32[4096,2,16]{2,1,0:T(2,128)} %bitcast.388) | data formatting | bytes 1048576
  162.9 6.4 %all-to-all-start.3 = ((f32[8,1,16384]{2,1,0:T(1,128)}), f32[8,1,16384]{2,1,0:T(1,128)S(1)}, u32[]{:S(2)}, u32[]{:S(2)}) async-start(f32[8,1,16384]{2,1,0:T(1,128)} %reshape.563), calls=%async_computation.3 | async-start | bytes 1048576 | tf_op jit(solution)/shard_map/all_to_all | solution.py:163
  169.3 12.7 %all-to-all-done.3 = f32[8,1,16384]{2,1,0:T(1,128)S(1)} async-done(((f32[8,1,16384]{2,1,0:T(1,128)}), f32[8,1,16384]{2,1,0:T(1,128)S(1)}, u32[]{:S(2)}, u32[]{:S(2)}) %all-to-all-start.3) | async-done | bytes 524320 | tf_op jit(solution)/shard_map/all_to_all | solution.py:163
  183.9 7.6 %reshape.564 = f32[4096,2,16]{2,1,0:T(2,128)} reshape(f32[8,16384]{1,0:T(8,128)S(1)} %reduce.1) | data formatting | bytes 1048576
  191.5 5.1 %copy.371 = f32[2,16,8,512]{3,1,2,0:T(8,128)S(1)} copy(f32[2,16,8,512]{1,0,3,2:T(2,128)} %bitcast.389) | data formatting | bytes 1048576 | tf_op jit(solution)/shard_map/all_to_all | solution.py:163
  198.3 26.8 %all_to_all.133 = f32[2,64,8,128]{3,2,0,1:T(8,128)S(1)} all-to-all(f32[2,64,8,128]{3,2,0,1:T(8,128)S(1)} %pad_maximum_fusion.3), channel_id=1, replica_groups=mesh['ha'=8,'az'=64] {'az'}, dimensions={1} | all-to-all | bytes 1048576 | tf_op jit(solution)/shard_map/all_to_all | solution.py:145
  228.3 7.7 %copy.298 = f32[2,8,8192]{1,0,2:T(2,128)} copy(f32[2,8,8192]{2,1,0:T(8,128)S(1)} %pad_maximum_fusion.4) | data formatting | bytes 1048576 | tf_op jit(solution)/shard_map/stack | solution.py:133
  236.0 13.0 %reshape.565 = f32[64,1,2048]{2,1,0:T(1,128)S(1)} reshape(f32[8192,2,8]{2,1,0:T(2,128)} %bitcast.386) | data formatting | bytes 1048576
  248.9 25.9 %all_to_all.134 = f32[64,1,2048]{2,1,0:T(1,128)S(1)} all-to-all(f32[64,1,2048]{2,1,0:T(1,128)S(1)} %reshape.565), channel_id=1, replica_groups=mesh['ha'=8,'az'=64] {'az'}, dimensions={0} | all-to-all | bytes 1048576 | tf_op jit(solution)/shard_map/all_to_all | solution.py:150
  276.7 14.1 %reshape.566 = f32[8192,2,8]{2,1,0:T(2,128)} reshape(f32[64,2048]{1,0:T(8,128)S(1)} %reduce.2) | data formatting | bytes 1048576
  290.8 9.2 %copy.376 = f32[2,8,64,128]{3,1,2,0:T(8,128)S(1)} copy(f32[2,8,64,128]{1,0,3,2:T(2,128)} %bitcast.387) | data formatting | bytes 1048576 | tf_op jit(solution)/shard_map/all_to_all | solution.py:150
  301.0 7.0 %all-to-all-start.6 = ((f32[2,128,512]{2,0,1:T(2,128)}), f32[2,128,512]{2,0,1:T(2,128)S(1)}, u32[]{:S(2)}, u32[]{:S(2)}) async-start(f32[2,128,512]{2,0,1:T(2,128)} %copy.301), calls=%async_computation.6 | async-start | bytes 1048576 | tf_op jit(solution)/shard_map/all_to_all | solution.py:159
  308.9 13.5 %all-to-all-done.6 = f32[2,128,512]{2,0,1:T(2,128)S(1)} async-done(((f32[2,128,512]{2,0,1:T(2,128)}), f32[2,128,512]{2,0,1:T(2,128)S(1)}, u32[]{:S(2)}, u32[]{:S(2)}) %all-to-all-start.6) | async-done | bytes 524320 | tf_op jit(solution)/shard_map/all_to_all | solution.py:159
  333.5 7.9 %reshape.567 = f32[8,1,16384]{2,1,0:T(1,128)} reshape(f32[4096,2,16]{2,1,0:T(2,128)} %bitcast.390) | data formatting | bytes 1048576
  341.3 6.3 %all-to-all-start.7 = ((f32[8,1,16384]{2,1,0:T(1,128)}), f32[8,1,16384]{2,1,0:T(1,128)S(1)}, u32[]{:S(2)}, u32[]{:S(2)}) async-start(f32[8,1,16384]{2,1,0:T(1,128)} %reshape.567), calls=%async_computation.7 | async-start | bytes 1048576 | tf_op jit(solution)/shard_map/all_to_all | solution.py:163
  347.9 12.5 %all-to-all-done.7 = f32[8,1,16384]{2,1,0:T(1,128)S(1)} async-done(((f32[8,1,16384]{2,1,0:T(1,128)}), f32[8,1,16384]{2,1,0:T(1,128)S(1)}, u32[]{:S(2)}, u32[]{:S(2)}) %all-to-all-start.7) | async-done | bytes 524320 | tf_op jit(solution)/shard_map/all_to_all | solution.py:163
  362.3 7.6 %reshape.568 = f32[4096,2,16]{2,1,0:T(2,128)} reshape(f32[8,16384]{1,0:T(8,128)S(1)} %reduce.3) | data formatting | bytes 1048576
  369.9 5.2 %copy.382 = f32[2,16,8,512]{3,1,2,0:T(8,128)S(1)} copy(f32[2,16,8,512]{1,0,3,2:T(2,128)} %bitcast.391) | data formatting | bytes 1048576 | tf_op jit(solution)/shard_map/all_to_all | solution.py:163
  382.0 12.0 %collective-permute-start.1 = (f32[128,15]{0,1:T(8,128)S(1)}, f32[128,15]{0,1:T(8,128)S(1)}, u32[]{:S(2)}, u32[]{:S(2)}) collective-permute-start(f32[128,15]{0,1:T(8,128)S(1)} %get-tuple-element.63), channel_id=1, source_target_pairs={{1,0},{2,1},{3,2},{4,3},{5,4},{6,5},{7,6},{8,7},{9,8},{10,9},{11,1... | collective-permute-start | bytes 23048 | tf_op jit(solution)/shard_map/ppermute | solution.py:27
  400.0 10.1 %collective-permute-start.3 = (f32[128,15]{0,1:T(8,128)S(1)}, f32[128,15]{0,1:T(8,128)S(1)}, u32[]{:S(2)}, u32[]{:S(2)}) collective-permute-start(f32[128,15]{0,1:T(8,128)S(1)} %get-tuple-element.61), channel_id=1, source_target_pairs={{1,0},{2,1},{3,2},{4,3},{5,4},{6,5},{7,6},{8,7},{9,8},{10,9},{11,1... | collective-permute-start | bytes 23048 | tf_op jit(solution)/shard_map/ppermute | solution.py:27
  415.5 12.3 %collective-permute-start.5 = (f32[128,15]{0,1:T(8,128)S(1)}, f32[128,15]{0,1:T(8,128)S(1)}, u32[]{:S(2)}, u32[]{:S(2)}) collective-permute-start(f32[128,15]{0,1:T(8,128)S(1)} %get-tuple-element.67), channel_id=1, source_target_pairs={{1,0},{2,1},{3,2},{4,3},{5,4},{6,5},{7,6},{8,7},{9,8},{10,9},{11,1... | collective-permute-start | bytes 23048 | tf_op jit(solution)/shard_map/ppermute | solution.py:27
  431.5 12.3 %collective-permute-start.7 = (f32[128,15]{0,1:T(8,128)S(1)}, f32[128,15]{0,1:T(8,128)S(1)}, u32[]{:S(2)}, u32[]{:S(2)}) collective-permute-start(f32[128,15]{0,1:T(8,128)S(1)} %get-tuple-element.65), channel_id=1, source_target_pairs={{1,0},{2,1},{3,2},{4,3},{5,4},{6,5},{7,6},{8,7},{9,8},{10,9},{11,1... | collective-permute-start | bytes 23048 | tf_op jit(solution)/shard_map/ppermute | solution.py:27
  (159 shorter events, 64.7 us)
Async XLA Ops:
  7.2 189.7 %copy-start = (f32[16,4096]{1,0:T(8,128)S(1)}, f32[16,4096]{1,0:T(8,128)}, u32[]{:S(2)}) copy-start(f32[16,4096]{1,0:T(8,128)} %param.11) | copy-start | bytes 786436
  9.1 33.9 %all-to-all-start = ((f32[2,64,8,128]{3,2,0,1:T(8,128)}), f32[2,64,8,128]{3,2,0,1:T(8,128)S(1)}, u32[]{:S(2)}, u32[]{:S(2)}) async-start(f32[2,64,8,128]{3,2,0,1:T(8,128)} %copy.267), calls=%async_computation | async-start | bytes 1048576 | tf_op jit(solution)/shard_map/all_to_all | solution.py:145
  120.8 23.1 %all-to-all-start.2 = ((f32[2,128,512]{2,0,1:T(2,128)}), f32[2,128,512]{2,0,1:T(2,128)S(1)}, u32[]{:S(2)}, u32[]{:S(2)}) async-start(f32[2,128,512]{2,0,1:T(2,128)} %copy.275), calls=%async_computation.2 | async-start | bytes 1048576 | tf_op jit(solution)/shard_map/all_to_all | solution.py:159
  162.9 19.1 %all-to-all-start.3 = ((f32[8,1,16384]{2,1,0:T(1,128)}), f32[8,1,16384]{2,1,0:T(1,128)S(1)}, u32[]{:S(2)}, u32[]{:S(2)}) async-start(f32[8,1,16384]{2,1,0:T(1,128)} %reshape.563), calls=%async_computation.3 | async-start | bytes 1048576 | tf_op jit(solution)/shard_map/all_to_all | solution.py:163
  183.9 12.9 %copy-start.4 = (s32[128]{0:T(128)S(1)}, s32[128]{0:T(128)}, u32[]{:S(2)}) copy-start(s32[128]{0:T(128)} %param.9) | copy-start | bytes 1540
  183.9 12.9 %copy-start.5 = (s32[128]{0:T(128)S(1)}, s32[128]{0:T(128)}, u32[]{:S(2)}) copy-start(s32[128]{0:T(128)} %param.10) | copy-start | bytes 1540
  301.0 21.3 %all-to-all-start.6 = ((f32[2,128,512]{2,0,1:T(2,128)}), f32[2,128,512]{2,0,1:T(2,128)S(1)}, u32[]{:S(2)}, u32[]{:S(2)}) async-start(f32[2,128,512]{2,0,1:T(2,128)} %copy.301), calls=%async_computation.6 | async-start | bytes 1048576 | tf_op jit(solution)/shard_map/all_to_all | solution.py:159
  308.0 70.5 %all-gather.5.cloned.1.call-start = ((), (), s32[]{:S(2)}) async-start(), calls=%async_computation.8 | async-start | bytes 1179648 | tf_op jit(solution)/shard_map/all_gather | solution.py:10
  341.3 19.1 %all-to-all-start.7 = ((f32[8,1,16384]{2,1,0:T(1,128)}), f32[8,1,16384]{2,1,0:T(1,128)S(1)}, u32[]{:S(2)}, u32[]{:S(2)}) async-start(f32[8,1,16384]{2,1,0:T(1,128)} %reshape.567), calls=%async_computation.7 | async-start | bytes 1048576 | tf_op jit(solution)/shard_map/all_to_all | solution.py:163
  347.6 64.3 %all-gather.7.cloned.1.call-start = ((), (), s32[]{:S(2)}) async-start(), calls=%async_computation.9 | async-start | bytes 1179648 | tf_op jit(solution)/shard_map/all_gather | solution.py:10
  369.9 7.5 %copy-start.6 = (f32[63]{0:T(128)S(1)}, f32[63]{0:T(128)}, u32[]{:S(2)}) copy-start(f32[63]{0:T(128)} %param.13) | copy-start | bytes 760
  369.9 8.0 %copy-start.7 = (f32[31]{0:T(128)S(1)}, f32[31]{0:T(128)}, u32[]{:S(2)}) copy-start(f32[31]{0:T(128)} %param.14) | copy-start | bytes 376
  369.9 9.9 %copy-start.2 = (s32[128,128]{1,0:T(8,128)S(1)}, s32[128,128]{1,0:T(8,128)}, u32[]{:S(2)}) copy-start(s32[128,128]{1,0:T(8,128)} %param.12) | copy-start | bytes 196612
  369.9 24.2 %copy-start.3 = (f32[2,128,128]{2,1,0:T(8,128)S(1)}, f32[2,128,128]{2,1,0:T(8,128)}, u32[]{:S(2)}) copy-start(f32[2,128,128]{2,1,0:T(8,128)} %param.15) | copy-start | bytes 393220
  375.3 71.3 %copy-start.1 = (f32[16,4096]{1,0:T(8,128)S(1)}, f32[16,4096]{1,0:T(8,128)}, u32[]{:S(2)}) copy-start(f32[16,4096]{1,0:T(8,128)} %param.11) | copy-start | bytes 786436
  380.1 14.1 %collective-permute-start = (f32[128,15]{0,1:T(8,128)S(1)}, f32[128,15]{0,1:T(8,128)S(1)}, u32[]{:S(2)}, u32[]{:S(2)}) collective-permute-start(f32[128,15]{0,1:T(8,128)S(1)} %get-tuple-element.62), channel_id=1, source_target_pairs={{0,1},{1,2},{2,3},{3,4},{4,5},{5,6},{6,7},{7,8},{8,9},{9,10},{10,1... | collective-permute-start | bytes 23048 | tf_op jit(solution)/shard_map/ppermute | solution.py:25
  382.0 13.4 %collective-permute-start.1 = (f32[128,15]{0,1:T(8,128)S(1)}, f32[128,15]{0,1:T(8,128)S(1)}, u32[]{:S(2)}, u32[]{:S(2)}) collective-permute-start(f32[128,15]{0,1:T(8,128)S(1)} %get-tuple-element.63), channel_id=1, source_target_pairs={{1,0},{2,1},{3,2},{4,3},{5,4},{6,5},{7,6},{8,7},{9,8},{10,9},{11,1... | collective-permute-start | bytes 23048 | tf_op jit(solution)/shard_map/ppermute | solution.py:27
  395.9 14.4 %collective-permute-start.2 = (f32[128,15]{0,1:T(8,128)S(1)}, f32[128,15]{0,1:T(8,128)S(1)}, u32[]{:S(2)}, u32[]{:S(2)}) collective-permute-start(f32[128,15]{0,1:T(8,128)S(1)} %get-tuple-element.60), channel_id=1, source_target_pairs={{0,1},{1,2},{2,3},{3,4},{4,5},{5,6},{6,7},{7,8},{8,9},{9,10},{10,1... | collective-permute-start | bytes 23048 | tf_op jit(solution)/shard_map/ppermute | solution.py:25
  400.0 11.5 %collective-permute-start.3 = (f32[128,15]{0,1:T(8,128)S(1)}, f32[128,15]{0,1:T(8,128)S(1)}, u32[]{:S(2)}, u32[]{:S(2)}) collective-permute-start(f32[128,15]{0,1:T(8,128)S(1)} %get-tuple-element.61), channel_id=1, source_target_pairs={{1,0},{2,1},{3,2},{4,3},{5,4},{6,5},{7,6},{8,7},{9,8},{10,9},{11,1... | collective-permute-start | bytes 23048 | tf_op jit(solution)/shard_map/ppermute | solution.py:27
  413.5 14.5 %collective-permute-start.4 = (f32[128,15]{0,1:T(8,128)S(1)}, f32[128,15]{0,1:T(8,128)S(1)}, u32[]{:S(2)}, u32[]{:S(2)}) collective-permute-start(f32[128,15]{0,1:T(8,128)S(1)} %get-tuple-element.66), channel_id=1, source_target_pairs={{0,1},{1,2},{2,3},{3,4},{4,5},{5,6},{6,7},{7,8},{8,9},{9,10},{10,1... | collective-permute-start | bytes 23048 | tf_op jit(solution)/shard_map/ppermute | solution.py:25
  415.5 13.7 %collective-permute-start.5 = (f32[128,15]{0,1:T(8,128)S(1)}, f32[128,15]{0,1:T(8,128)S(1)}, u32[]{:S(2)}, u32[]{:S(2)}) collective-permute-start(f32[128,15]{0,1:T(8,128)S(1)} %get-tuple-element.67), channel_id=1, source_target_pairs={{1,0},{2,1},{3,2},{4,3},{5,4},{6,5},{7,6},{8,7},{9,8},{10,9},{11,1... | collective-permute-start | bytes 23048 | tf_op jit(solution)/shard_map/ppermute | solution.py:27
  429.6 15.1 %collective-permute-start.6 = (f32[128,15]{0,1:T(8,128)S(1)}, f32[128,15]{0,1:T(8,128)S(1)}, u32[]{:S(2)}, u32[]{:S(2)}) collective-permute-start(f32[128,15]{0,1:T(8,128)S(1)} %get-tuple-element.64), channel_id=1, source_target_pairs={{0,1},{1,2},{2,3},{3,4},{4,5},{5,6},{6,7},{7,8},{8,9},{9,10},{10,1... | collective-permute-start | bytes 23048 | tf_op jit(solution)/shard_map/ppermute | solution.py:25
  431.5 13.7 %collective-permute-start.7 = (f32[128,15]{0,1:T(8,128)S(1)}, f32[128,15]{0,1:T(8,128)S(1)}, u32[]{:S(2)}, u32[]{:S(2)}) collective-permute-start(f32[128,15]{0,1:T(8,128)S(1)} %get-tuple-element.65), channel_id=1, source_target_pairs={{1,0},{2,1},{3,2},{4,3},{5,4},{6,5},{7,6},{8,7},{9,8},{10,9},{11,1... | collective-permute-start | bytes 23048 | tf_op jit(solution)/shard_map/ppermute | solution.py:27
Sparse Core Ops, SparseCore 0:
  310.8 29.5 all-gather.4
  377.5 28.5 all-gather.6
